TPU v7x, 32 devices: a whole 2x2x4 slice. The times are simulated.
32 devices in a mesh: row: 4 (over z), col: 8 (over y, x, core).
Axes of the slice: x: 2, y: 2, z: 4, core: 2. Of those that a mesh axis runs over, the one named last changes fastest.
Arguments:
- features: bfloat16 [8192, 512], P(('row', 'col')), may hold values from -6 to 6
- tile_values: bfloat16 [32, 16, 128, 128], P(('row', 'col')), may hold values from -0.21875 to 0.21875
- tile_blocks: int32 [32, 16, 2], P(('row', 'col')), may hold values from 0 to 63, as said below
- tile_count: int32 [32], P(('row', 'col')), may hold values from 1 to 16, as said below
- needed: int32 [32, 4], P(('row', 'col')), may hold values from 0 to 1
- weight_one: bfloat16 [512, 512], replicated, may hold values from -0.25 to 0.25
- weight_two: bfloat16 [512, 512], replicated, may hold values from -0.25 to 0.25
Outputs:
- nodes_out: bfloat16 [8192, 512], P(('row', 'col'))
Inputs may be any that keep to these rules, and one draw needn't show every extreme that they name: `tile_blocks`: every row block of device d lies among the row blocks owned by the devices that share its index along row; for each device e along col in device d's row, all live or dead tiles of device d whose row block is owned by e name the same one of e's 2 blocks; the last device's first slot names the last block. `tile_count`: some device in every draw has all 16 slots live.
All inputs are finite; a program needn't handle non-finite values.
Results may differ from a plain program's by a relative error of at most 0.017.
Values may be sent and summed in bfloat16 or wider, within the bound.
No kernel may reach another device: no remote copies, remote signals or barrier semaphores. Data moves between devices by JAX's collectives and lax.ppermute only.
A program may use at most 64 MiB of HBM per device.

v0:
```python
import jax
import jax.numpy as jnp
from jax import lax
from jax.sharding import PartitionSpec as P


def body(features, tile_values, tile_blocks, tile_count, needed, weight_one, weight_two):
    col_count = lax.axis_size("col")
    adjacency = tile_values[0]
    blocks_here = tile_blocks[0]
    tile_slots = adjacency.shape[0]
    tile_size = adjacency.shape[1]
    feat_width = features.shape[1]
    per_device = features.shape[0] // tile_size
    alive_mask = jnp.arange(tile_slots) < tile_count[0]
    source_owner = blocks_here[:, 1]
    wanted = needed[0]
    target = blocks_here[:, 0] // per_device % col_count
    local_block = blocks_here[:, 0] % per_device
    dest_hit = (target[:, None] == jnp.arange(col_count)[None, :]) & alive_mask[:, None]
    dest_weights = dest_hit.astype(jnp.bfloat16)
    both_weights = jnp.concatenate([dest_weights, dest_weights], axis=0)
    send_block = jnp.max(jnp.where(dest_hit, local_block[:, None], 0), axis=0)
    hidden = features
    for layer_index, weight in enumerate((weight_one, weight_two)):
        owned = hidden.reshape(per_device, tile_size, feat_width)
        panel_rows = lax.all_gather(owned, "row", axis=0, tiled=True)
        operands = panel_rows[source_owner * per_device + wanted[source_owner]]
        products = jnp.einsum(
            "tmk,tkf->tmf", adjacency, operands, preferred_element_type=jnp.float32
        )
        upper_part = products.astype(jnp.bfloat16)
        lower_part = (products - upper_part.astype(jnp.float32)).astype(jnp.bfloat16)
        stacked = jnp.concatenate([upper_part, lower_part], axis=0)
        partial_value = jnp.einsum(
            "tc,tmf->cmf", both_weights, stacked, preferred_element_type=jnp.float32
        )
        partial_value = partial_value.astype(jnp.bfloat16)
        arrived_parts = lax.all_to_all(
            partial_value, "col", split_axis=0, concat_axis=0, tiled=True
        )
        picked = lax.all_to_all(send_block, "col", split_axis=0, concat_axis=0, tiled=True)
        chooser = (picked[:, None] == jnp.arange(per_device)[None, :]).astype(jnp.bfloat16)
        summed = jnp.einsum(
            "sb,smf->bmf", chooser, arrived_parts, preferred_element_type=jnp.float32
        )
        mixed = summed.astype(jnp.bfloat16).reshape(per_device * tile_size, feat_width)
        result = jnp.dot(mixed, weight, preferred_element_type=jnp.float32)
        if layer_index == 0:
            hidden = jnp.maximum(result, 0.0).astype(jnp.bfloat16)
        else:
            hidden = result.astype(jnp.bfloat16)
    return hidden


def solution(mesh):
    placed = (
        P(("row", "col"), None),
        P(("row", "col"), None, None, None),
        P(("row", "col"), None, None),
        P(("row", "col")),
        P(("row", "col"), None),
        P(),
        P(),
    )
    return jax.shard_map(
        body, mesh=mesh, in_specs=placed, out_specs=P(("row", "col"), None), check_vma=False
    )
```

profile of v0, /device:TPU:0, one launch (start us, length us, event | category | flops | bytes accessed | tf_op | source)
XLA Modules:
  0.0 147.8 jit_solution(7393868171918821235)
XLA Ops:
  6.5 0.7 all-gather.3.cloned.1.call-update
  8.6 0.8 fusion.12
  10.2 5.2 %all-to-all-start = ((s32[8,1,1]{2,1,0:T(1,128)}), s32[8,1,1]{2,1,0:T(1,128)S(1)}, u32[]{:S(2)}, u32[]{:S(2)}) async-start(s32[8,1,1]{2,1,0:T(1,128)} %copy.23), calls=%async_computation | async-start | bytes 8192 | tf_op jit(solution)/shard_map/all_to_all | solution.py:42
  15.4 1.3 gather_fusion
  17.4 22.2 %all-gather.3.cloned.1.call-done = bf16[8,128,512]{2,1,0:T(8,128)(2,1)} async-done(((bf16[2,128,512]{2,1,0:T(8,128)(2,1)}), bf16[8,128,512]{2,1,0:T(8,128)(2,1)}) %all-gather.3.cloned.1.call-update) | async-done | bytes 1048592 | tf_op jit(solution)/shard_map/all_gather | solution.py:27
  39.6 1.9 %gather_fusion.1 = bf16[16,128,512]{2,1,0:T(8,128)(2,1)S(1)} fusion(bf16[8,128,512]{2,1,0:T(8,128)(2,1)} %all-gather.3.cloned.1.call-done, s32[1024]{0:T(1024)S(1)} %pad_clamp_fusion), kind=kCustom, calls=%fused_computation.1 | custom fusion | bytes 4194368 | tf_op jit(solution)/shard_map/gather | solution.py:28
  41.5 1.0 fusion.1
  42.5 2.3 %pad_maximum_fusion = bf16[32,128,512]{1,2,0:T(8,128)(2,1)} fusion(bf16[16,128,512]{1,2,0:T(8,128)(2,1)S(1)} %get-tuple-element.9, bf16[16,128,512]{1,2,0:T(8,128)(2,1)S(1)} %get-tuple-element.10), kind=kLoop, calls=%fused_computation.3 | loop fusion | flops 2097152 | bytes 8388608 | tf_op jit(solution)/shard_map/concatenate | solution.py:34
  44.8 8.0 %copy.25 = bf16[32,128,512]{2,0,1:T(8,128)(2,1)} copy(bf16[32,128,512]{1,2,0:T(8,128)(2,1)} %pad_maximum_fusion) | data formatting | bytes 8388608 | tf_op jit(solution)/shard_map/concatenate | solution.py:34
  52.8 2.9 %convolution_convert_fusion.1 = bf16[8,128,512]{2,0,1:T(8,128)(2,1)S(1)} fusion(bf16[32,128,512]{2,0,1:T(8,128)(2,1)} %copy.25, pred[16,8]{0,1:T(8,128)(4,1)S(1)} %fusion.9), kind=kOutput, calls=%fused_computation.12 | convolution fusion | flops 34078976 | bytes 5243008 | tf_op jit(solution)/shard_map/tc,tmf->cmf/dot_general | solution.py:35
  55.7 1.3 copy.26
  57.0 3.8 %all-to-all-start.1 = ((bf16[8,128,512]{2,1,0:T(8,128)(2,1)}), bf16[8,128,512]{2,1,0:T(8,128)(2,1)S(1)}, u32[]{:S(2)}, u32[]{:S(2)}) async-start(bf16[8,128,512]{2,1,0:T(8,128)(2,1)} %copy.26), calls=%async_computation.1 | async-start | bytes 2097152 | tf_op jit(solution)/shard_map/all_to_all | solution.py:39
  61.0 15.1 %all-to-all-done.1 = bf16[8,128,512]{2,1,0:T(8,128)(2,1)S(1)} async-done(((bf16[8,128,512]{2,1,0:T(8,128)(2,1)}), bf16[8,128,512]{2,1,0:T(8,128)(2,1)S(1)}, u32[]{:S(2)}, u32[]{:S(2)}) %all-to-all-start.1) | async-done | bytes 1048608 | tf_op jit(solution)/shard_map/all_to_all | solution.py:39
  76.2 0.7 convolution_convert_fusion.4
  77.0 1.0 fusion.2
  78.0 25.8 %all-gather.5.cloned.1.call-done = bf16[8,128,512]{2,1,0:T(8,128)(2,1)} async-done(((bf16[2,128,512]{2,1,0:T(8,128)(2,1)}), bf16[8,128,512]{2,1,0:T(8,128)(2,1)}) %all-gather.5.cloned.1.call-update) | async-done | bytes 1048592 | tf_op jit(solution)/shard_map/all_gather | solution.py:27
  103.8 1.9 %gather_fusion.2 = bf16[16,128,512]{2,1,0:T(8,128)(2,1)S(1)} fusion(bf16[8,128,512]{2,1,0:T(8,128)(2,1)} %all-gather.5.cloned.1.call-done, s32[1024]{0:T(1024)S(1)} %pad_clamp_fusion), kind=kCustom, calls=%fused_computation.2 | custom fusion | bytes 4194368 | tf_op jit(solution)/shard_map/gather | solution.py:28
  105.7 1.0 fusion
  106.7 2.3 %pad_maximum_fusion.1 = bf16[32,128,512]{1,2,0:T(8,128)(2,1)} fusion(bf16[16,128,512]{1,2,0:T(8,128)(2,1)S(1)} %get-tuple-element.5, bf16[16,128,512]{1,2,0:T(8,128)(2,1)S(1)} %get-tuple-element.6), kind=kLoop, calls=%fused_computation.4 | loop fusion | flops 2097152 | bytes 8388608 | tf_op jit(solution)/shard_map/concatenate | solution.py:34
  109.0 8.0 %copy.30 = bf16[32,128,512]{2,0,1:T(8,128)(2,1)} copy(bf16[32,128,512]{1,2,0:T(8,128)(2,1)} %pad_maximum_fusion.1) | data formatting | bytes 8388608 | tf_op jit(solution)/shard_map/concatenate | solution.py:34
  117.0 2.9 %convolution_convert_fusion = bf16[8,128,512]{2,0,1:T(8,128)(2,1)S(1)} fusion(bf16[32,128,512]{2,0,1:T(8,128)(2,1)} %copy.30, pred[16,8]{0,1:T(8,128)(4,1)S(1)} %fusion.9), kind=kOutput, calls=%fused_computation.11 | convolution fusion | flops 34078976 | bytes 5243008 | tf_op jit(solution)/shard_map/tc,tmf->cmf/dot_general | solution.py:35
  120.2 18.9 %all_to_all.20 = bf16[8,128,512]{2,1,0:T(8,128)(2,1)S(1)} all-to-all(bf16[8,128,512]{2,1,0:T(8,128)(2,1)S(1)} %copy.31), channel_id=1, replica_groups=mesh['row'=4,'col'=8] {'col'}, dimensions={0} | all-to-all | bytes 2097152 | tf_op jit(solution)/shard_map/all_to_all | solution.py:39
  139.2 0.7 convolution_convert_fusion.3
  140.0 1.0 convolution_convert_fusion.2
  (22 shorter events, 2.9 us)
Async XLA Ops:
  6.5 35.0 %copy-start = (bf16[1,16,128,128]{3,2,1,0:T(8,128)(2,1)S(1)}, bf16[1,16,128,128]{3,2,1,0:T(8,128)(2,1)}, u32[]{:S(2)}) copy-start(bf16[1,16,128,128]{3,2,1,0:T(8,128)(2,1)} %param.8) | copy-start | bytes 1572868
  6.5 33.1 %all-gather.3.cloned.1.call-start = ((), (), s32[]{:S(2)}) async-start(), calls=%async_computation.3 | async-start | bytes 1310720 | tf_op jit(solution)/shard_map/all_gather | solution.py:27
  10.2 46.8 %all-to-all-start = ((s32[8,1,1]{2,1,0:T(1,128)}), s32[8,1,1]{2,1,0:T(1,128)S(1)}, u32[]{:S(2)}, u32[]{:S(2)}) async-start(s32[8,1,1]{2,1,0:T(1,128)} %copy.23), calls=%async_computation | async-start | bytes 8192 | tf_op jit(solution)/shard_map/all_to_all | solution.py:42
  57.0 20.0 %copy-start.1 = (bf16[512,512]{1,0:T(8,128)(2,1)S(1)}, bf16[512,512]{1,0:T(8,128)(2,1)}, u32[]{:S(2)}) copy-start(bf16[512,512]{1,0:T(8,128)(2,1)} %param.12) | copy-start | bytes 1572868
  57.0 19.2 %all-to-all-start.1 = ((bf16[8,128,512]{2,1,0:T(8,128)(2,1)}), bf16[8,128,512]{2,1,0:T(8,128)(2,1)S(1)}, u32[]{:S(2)}, u32[]{:S(2)}) async-start(bf16[8,128,512]{2,1,0:T(8,128)(2,1)} %copy.26), calls=%async_computation.1 | async-start | bytes 2097152 | tf_op jit(solution)/shard_map/all_to_all | solution.py:39
  60.8 43.0 %all-gather.5.cloned.1.call-start = ((), (), s32[]{:S(2)}) async-start(), calls=%async_computation.4 | async-start | bytes 1310720 | tf_op jit(solution)/shard_map/all_gather | solution.py:27
  120.2 19.7 %copy-start.2 = (bf16[512,512]{1,0:T(8,128)(2,1)S(1)}, bf16[512,512]{1,0:T(8,128)(2,1)}, u32[]{:S(2)}) copy-start(bf16[512,512]{1,0:T(8,128)(2,1)} %param.13) | copy-start | bytes 1572868
Sparse Core Ops, SparseCore 0:
  8.9 30.6 all-gather.2
  78.1 25.6 all-gather.4
where the time goes:
time: 149 us; the launch traced here: 148 us
  waiting for transfers between devices  63.9 us (43%)
  local copies, waits for them, and re-layouts  23.4 us (16%)
  blocking collectives  18.9 us (13%)
  between operations  14.2 us (10%)
  matrix products  11.3 us (8%)
  starting transfers between devices  9 us (6%)
  other arithmetic  7.17 us (5%)
    all_gather x2, waiting for transfers between devices, body(): panel_rows = lax.all_gather(owned, 'row', axis=0, tiled=True)  48 us
    all_to_all x1, blocking collectives, body(): lax.all_to_all(partial_value, 'col', split_axis=0, concat_axis=0, tiled=T...  18.9 us
    concatenate x2, local copies, waits for them, and re-layouts, body(): stacked = jnp.concatenate([upper_part, lower_part], axis=0)  15.9 us
    all_to_all x1, waiting for transfers between devices, body(): lax.all_to_all(partial_value, 'col', split_axis=0, concat_axis=0, tiled=T...  15.1 us
    dot_general x2, matrix products, body(): jnp.einsum('tc,tmf->cmf', both_weights, stacked, preferred_element_type=j...  5.81 us
    all_to_all x1, starting transfers between devices, body(): lax.all_to_all(send_block, 'col', split_axis=0, concat_axis=0, tiled=True)  5.17 us
    gather x3, local copies, waits for them, and re-layouts, body(): operands = panel_rows[source_owner * per_device + wanted[source_owner]]  5.12 us
    concatenate x2, other arithmetic, body(): stacked = jnp.concatenate([upper_part, lower_part], axis=0)  4.64 us
  transfers between devices with their start and end apart: 4, of which 3 were waited for; matrix products, arithmetic and copies ran while one was open for 15% of the time, Pallas kernels for 0%

commit v1 on v0

--- a/solution.py
+++ b/solution.py
@@ -24,7 +24,26 @@
     hidden = features
     for layer_index, weight in enumerate((weight_one, weight_two)):
         owned = hidden.reshape(per_device, tile_size, feat_width)
-        panel_rows = lax.all_gather(owned, "row", axis=0, tiled=True)
+        carry_out = lax.axis_size("row")
+        part_now = lax.axis_index("row")
+        inter, prior, k_now = (carry_out, part_now, owned.shape[0])
+        runs = [p * inter if i == 0 else p for i, p in enumerate(owned.shape)]
+        panel_rows = lax.dynamic_update_slice_in_dim(
+            jnp.zeros(runs, owned.dtype), owned, prior * k_now, axis=0
+        )
+        tall = state_now = owned
+        for rr in range(1, inter // 2 + 1):
+            tall = lax.ppermute(tall, "row", [(i, (i + 1) % inter) for i in range(inter)])
+            panel_rows = lax.dynamic_update_slice_in_dim(
+                panel_rows, tall, (prior - rr) % inter * k_now, axis=0
+            )
+            if 2 * rr < inter:
+                state_now = lax.ppermute(
+                    state_now, "row", [(i, (i - 1) % inter) for i in range(inter)]
+                )
+                panel_rows = lax.dynamic_update_slice_in_dim(
+                    panel_rows, state_now, (prior + rr) % inter * k_now, axis=0
+                )
         operands = panel_rows[source_owner * per_device + wanted[source_owner]]
         products = jnp.einsum(
             "tmk,tkf->tmf", adjacency, operands, preferred_element_type=jnp.float32

time: 149 us -> 124 us (0.83)
  waiting for transfers between devices: 63.9 us -> 40.9 us
  between operations: 14.2 us -> 0.94 us
  starting transfers between devices: 9 us -> 16.9 us
  matrix products: 11.3 us -> 13.7 us
  local copies, waits for them, and re-layouts: 23.4 us -> 24.9 us
    all_gather x2 -> x0, waiting for transfers between devices: 48 us -> none  [body(): panel_rows = lax.all_gather(owned, 'row', axis=0, tiled=True)]
    ppermute x0 -> x6, waiting for transfers between devices: none -> 25.7 us  [the longest x4 22.5 us: body(): lax.ppermute(tall, 'row', [(i, (i + 1) % inter) for i in range(inter)])]
    ppermute x0 -> x6, starting transfers between devices: none -> 9.04 us  [the longest x2 5.89 us: body(): lax.ppermute(state_now, 'row', [(i, (i - 1) % inter) for i in range(inter)])]
    dot_general x2, matrix products: 1.94 us -> 5.12 us  [body(): jnp.einsum('tmk,tkf->tmf', adjacency, operands, preferred_element_type=jn...]
  transfers between devices with their start and end apart: 4 -> 8, of which waited for: 3 -> 6; matrix products, arithmetic and copies ran while one was open for 15% -> 20% of each run, Pallas kernels for 0% -> 0%
where the time goes in v1:
time: 124 us
  waiting for transfers between devices  40.9 us (33%)
  local copies, waits for them, and re-layouts  24.9 us (20%)
  blocking collectives  19.1 us (15%)
  starting transfers between devices  16.9 us (14%)
  matrix products  13.7 us (11%)
  other arithmetic  7.16 us (6%)
    ppermute x4, waiting for transfers between devices, body(): lax.ppermute(tall, 'row', [(i, (i + 1) % inter) for i in range(inter)])  22.5 us
    all_to_all x1, blocking collectives, body(): lax.all_to_all(partial_value, 'col', split_axis=0, concat_axis=0, tiled=T...  19.1 us
    concatenate x2, local copies, waits for them, and re-layouts, body(): stacked = jnp.concatenate([upper_part, lower_part], axis=0)  15.9 us
    all_to_all x1, waiting for transfers between devices, body(): lax.all_to_all(partial_value, 'col', split_axis=0, concat_axis=0, tiled=T...  15.2 us
    ppermute x2, starting transfers between devices, body(): lax.ppermute(state_now, 'row', [(i, (i - 1) % inter) for i in range(inter)])  5.89 us
    dot_general x2, matrix products, body(): jnp.einsum('tc,tmf->cmf', both_weights, stacked, preferred_element_type=j...  5.81 us
    gather x3, local copies, waits for them, and re-layouts, body(): operands = panel_rows[source_owner * per_device + wanted[source_owner]]  5.34 us
    dot_general x2, matrix products, body(): jnp.einsum('tmk,tkf->tmf', adjacency, operands, preferred_element_type=jn...  5.12 us
  transfers between devices with their start and end apart: 8, of which 6 were waited for; matrix products, arithmetic and copies ran while one was open for 20% of the time, Pallas kernels for 0%

profile of v1, /device:TPU:0, one launch (start us, length us, event | category | flops | bytes accessed | tf_op | source)
XLA Modules:
  0.0 123.6 jit_solution(3990507002772194064)
XLA Ops:
  0.0 3.0 %collective-permute-start = (bf16[2,128,512]{2,1,0:T(8,128)(2,1)}, bf16[2,128,512]{2,1,0:T(8,128)(2,1)S(1)}, u32[]{:S(2)}, u32[]{:S(2)}) collective-permute-start(bf16[2,128,512]{2,1,0:T(8,128)(2,1)} %bitcast.65), channel_id=1, source_target_pairs={{0,8},{8,16},{16,24},{24,0},{1,9},{9,17},{17,25},{25,1},{2,10},{10... | collective-permute-start | bytes 786440 | tf_op jit(solution)/shard_map/ppermute | solution.py:36
  3.0 2.1 %collective-permute-start.1 = (bf16[2,128,512]{2,1,0:T(8,128)(2,1)}, bf16[2,128,512]{2,1,0:T(8,128)(2,1)S(1)}, u32[]{:S(2)}, u32[]{:S(2)}) collective-permute-start(bf16[2,128,512]{2,1,0:T(8,128)(2,1)} %bitcast.66), channel_id=1, source_target_pairs={{0,24},{8,0},{16,8},{24,16},{1,25},{9,1},{17,9},{25,17},{2,26},{10... | collective-permute-start | bytes 786440 | tf_op jit(solution)/shard_map/ppermute | solution.py:41
  8.0 3.9 %all-to-all-start = ((s32[8,1,1]{2,1,0:T(1,128)}), s32[8,1,1]{2,1,0:T(1,128)S(1)}, u32[]{:S(2)}, u32[]{:S(2)}) async-start(s32[8,1,1]{2,1,0:T(1,128)} %copy.23), calls=%async_computation | async-start | bytes 8192 | tf_op jit(solution)/shard_map/all_to_all | solution.py:61
  11.9 1.3 %gather_fusion = s32[16]{0:T(128)S(1)} fusion(s32[4]{0:T(128)} %bitcast.59, s32[1024]{0:T(1024)S(1)} %pad_clamp_fusion.1), kind=kCustom, calls=%fused_computation | custom fusion | bytes 192 | tf_op jit(solution)/shard_map/gather | solution.py:47
  15.2 1.4 %collective-permute-done.1 = bf16[2,128,512]{2,1,0:T(8,128)(2,1)S(1)} collective-permute-done((bf16[2,128,512]{2,1,0:T(8,128)(2,1)}, bf16[2,128,512]{2,1,0:T(8,128)(2,1)S(1)}, u32[]{:S(2)}, u32[]{:S(2)}) %collective-permute-start.1) | collective-permute-done | bytes 262176 | tf_op jit(solution)/shard_map/ppermute | solution.py:41
  16.6 9.0 %collective-permute-done.2 = bf16[2,128,512]{2,1,0:T(8,128)(2,1)S(1)} collective-permute-done((bf16[2,128,512]{2,1,0:T(8,128)(2,1)S(1)}, bf16[2,128,512]{2,1,0:T(8,128)(2,1)S(1)}, u32[]{:S(2)}, u32[]{:S(2)}) %collective-permute-start.2) | collective-permute-done | bytes 262176 | tf_op jit(solution)/shard_map/ppermute | solution.py:36
  25.6 2.0 %gather_fusion.1 = bf16[16,128,512]{2,1,0:T(8,128)(2,1)} fusion(bf16[8,128,512]{2,1,0:T(8,128)(2,1)S(1)} %constant_dynamic-update-slice_fusion.4, s32[1024]{0:T(1024)S(1)} %pad_clamp_fusion), kind=kCustom, calls=%fused_computation.1 | custom fusion | bytes 4194368 | tf_op jit(solution)/shard_map/gather | solution.py:47
  27.6 2.6 %fusion.1 = (bf16[16,128,512]{1,2,0:T(8,128)(2,1)S(1)}, bf16[16,128,512]{1,2,0:T(8,128)(2,1)S(1)}) fusion(bf16[16,128,512]{2,1,0:T(8,128)(2,1)} %gather_fusion.1, bf16[1,16,128,128]{3,2,1,0:T(8,128)(2,1)S(1)} %copy-done), kind=kOutput, calls=%fused_computation.10 | convolution fusion | flops 272629760 | bytes 6815744 | tf_op jit(solution)/shard_map/tmk,tkf->tmf/dot_general | solution.py:48
  30.2 2.3 %pad_maximum_fusion = bf16[32,128,512]{1,2,0:T(8,128)(2,1)} fusion(bf16[16,128,512]{1,2,0:T(8,128)(2,1)S(1)} %get-tuple-element.9, bf16[16,128,512]{1,2,0:T(8,128)(2,1)S(1)} %get-tuple-element.10), kind=kLoop, calls=%fused_computation.3 | loop fusion | flops 2097152 | bytes 8388608 | tf_op jit(solution)/shard_map/concatenate | solution.py:53
  32.5 8.0 %copy.25 = bf16[32,128,512]{2,0,1:T(8,128)(2,1)} copy(bf16[32,128,512]{1,2,0:T(8,128)(2,1)} %pad_maximum_fusion) | data formatting | bytes 8388608 | tf_op jit(solution)/shard_map/concatenate | solution.py:53
  40.5 2.9 %convolution_convert_fusion.1 = bf16[8,128,512]{2,0,1:T(8,128)(2,1)S(1)} fusion(bf16[32,128,512]{2,0,1:T(8,128)(2,1)} %copy.25, pred[16,8]{0,1:T(8,128)(4,1)S(1)} %fusion.9), kind=kOutput, calls=%fused_computation.12 | convolution fusion | flops 34078976 | bytes 5243008 | tf_op jit(solution)/shard_map/tc,tmf->cmf/dot_general | solution.py:54
  43.4 1.3 %copy.26 = bf16[8,128,512]{2,1,0:T(8,128)(2,1)} copy(bf16[8,128,512]{2,0,1:T(8,128)(2,1)S(1)} %convolution_convert_fusion.1) | data formatting | bytes 2097152 | tf_op jit(solution)/shard_map/convert_element_type | solution.py:57
  44.7 4.0 %all-to-all-start.1 = ((bf16[8,128,512]{2,1,0:T(8,128)(2,1)}), bf16[8,128,512]{2,1,0:T(8,128)(2,1)S(1)}, u32[]{:S(2)}, u32[]{:S(2)}) async-start(bf16[8,128,512]{2,1,0:T(8,128)(2,1)} %copy.26), calls=%async_computation.1 | async-start | bytes 2097152 | tf_op jit(solution)/shard_map/all_to_all | solution.py:58
  48.9 15.2 %all-to-all-done.1 = bf16[8,128,512]{2,1,0:T(8,128)(2,1)S(1)} async-done(((bf16[8,128,512]{2,1,0:T(8,128)(2,1)}), bf16[8,128,512]{2,1,0:T(8,128)(2,1)S(1)}, u32[]{:S(2)}, u32[]{:S(2)}) %all-to-all-start.1) | async-done | bytes 1048608 | tf_op jit(solution)/shard_map/all_to_all | solution.py:58
  65.2 3.8 %collective-permute-start.4 = (bf16[2,128,512]{2,1,0:T(8,128)(2,1)S(1)}, bf16[2,128,512]{2,1,0:T(8,128)(2,1)S(1)}, u32[]{:S(2)}, u32[]{:S(2)}) collective-permute-start(bf16[2,128,512]{2,1,0:T(8,128)(2,1)S(1)} %bitcast.61), channel_id=1, source_target_pairs={{0,24},{8,0},{16,8},{24,16},{1,25},{9,1},{17,9},{25,17},{2,26},{10... | collective-permute-start | bytes 786440 | tf_op jit(solution)/shard_map/ppermute | solution.py:41
  69.1 7.3 %collective-permute-done.3 = bf16[2,128,512]{2,1,0:T(8,128)(2,1)S(1)} collective-permute-done((bf16[2,128,512]{2,1,0:T(8,128)(2,1)S(1)}, bf16[2,128,512]{2,1,0:T(8,128)(2,1)S(1)}, u32[]{:S(2)}, u32[]{:S(2)}) %collective-permute-start.3) | collective-permute-done | bytes 262176 | tf_op jit(solution)/shard_map/ppermute | solution.py:36
  76.5 1.7 %collective-permute-done.4 = bf16[2,128,512]{2,1,0:T(8,128)(2,1)S(1)} collective-permute-done((bf16[2,128,512]{2,1,0:T(8,128)(2,1)S(1)}, bf16[2,128,512]{2,1,0:T(8,128)(2,1)S(1)}, u32[]{:S(2)}, u32[]{:S(2)}) %collective-permute-start.4) | collective-permute-done | bytes 262176 | tf_op jit(solution)/shard_map/ppermute | solution.py:41
  78.3 6.2 %collective-permute-done.5 = bf16[2,128,512]{2,1,0:T(8,128)(2,1)S(1)} collective-permute-done((bf16[2,128,512]{2,1,0:T(8,128)(2,1)S(1)}, bf16[2,128,512]{2,1,0:T(8,128)(2,1)S(1)}, u32[]{:S(2)}, u32[]{:S(2)}) %collective-permute-start.5) | collective-permute-done | bytes 262176 | tf_op jit(solution)/shard_map/ppermute | solution.py:36
  84.6 2.0 %gather_fusion.2 = bf16[16,128,512]{2,1,0:T(8,128)(2,1)} fusion(bf16[8,128,512]{2,1,0:T(8,128)(2,1)S(1)} %constant_dynamic-update-slice_fusion, s32[1024]{0:T(1024)S(1)} %pad_clamp_fusion), kind=kCustom, calls=%fused_computation.2 | custom fusion | bytes 4194368 | tf_op jit(solution)/shard_map/gather | solution.py:47
  86.6 2.6 %fusion = (bf16[16,128,512]{1,2,0:T(8,128)(2,1)S(1)}, bf16[16,128,512]{1,2,0:T(8,128)(2,1)S(1)}) fusion(bf16[16,128,512]{2,1,0:T(8,128)(2,1)} %gather_fusion.2, bf16[1,16,128,128]{3,2,1,0:T(8,128)(2,1)S(1)} %copy-done), kind=kOutput, calls=%fused_computation.7 | convolution fusion | flops 272629760 | bytes 6815744 | tf_op jit(solution)/shard_map/tmk,tkf->tmf/dot_general | solution.py:48
  89.2 2.3 %pad_maximum_fusion.1 = bf16[32,128,512]{1,2,0:T(8,128)(2,1)} fusion(bf16[16,128,512]{1,2,0:T(8,128)(2,1)S(1)} %get-tuple-element.5, bf16[16,128,512]{1,2,0:T(8,128)(2,1)S(1)} %get-tuple-element.6), kind=kLoop, calls=%fused_computation.4 | loop fusion | flops 2097152 | bytes 8388608 | tf_op jit(solution)/shard_map/concatenate | solution.py:53
  91.5 8.0 %copy.30 = bf16[32,128,512]{2,0,1:T(8,128)(2,1)} copy(bf16[32,128,512]{1,2,0:T(8,128)(2,1)} %pad_maximum_fusion.1) | data formatting | bytes 8388608 | tf_op jit(solution)/shard_map/concatenate | solution.py:53
  99.4 2.9 %convolution_convert_fusion = bf16[8,128,512]{2,0,1:T(8,128)(2,1)S(1)} fusion(bf16[32,128,512]{2,0,1:T(8,128)(2,1)} %copy.30, pred[16,8]{0,1:T(8,128)(4,1)S(1)} %fusion.9), kind=kOutput, calls=%fused_computation.11 | convolution fusion | flops 34078976 | bytes 5243008 | tf_op jit(solution)/shard_map/tc,tmf->cmf/dot_general | solution.py:54
  102.7 19.1 %all_to_all.20 = bf16[8,128,512]{2,1,0:T(8,128)(2,1)S(1)} all-to-all(bf16[8,128,512]{2,1,0:T(8,128)(2,1)S(1)} %copy.31), channel_id=1, replica_groups=mesh['row'=4,'col'=8] {'col'}, dimensions={0} | all-to-all | bytes 2097152 | tf_op jit(solution)/shard_map/all_to_all | solution.py:58
  (38 shorter events, 7.8 us)
Async XLA Ops:
  0.0 27.6 %copy-start = (bf16[1,16,128,128]{3,2,1,0:T(8,128)(2,1)S(1)}, bf16[1,16,128,128]{3,2,1,0:T(8,128)(2,1)}, u32[]{:S(2)}) copy-start(bf16[1,16,128,128]{3,2,1,0:T(8,128)(2,1)} %param.8) | copy-start | bytes 1572868
  0.0 15.0 %collective-permute-start = (bf16[2,128,512]{2,1,0:T(8,128)(2,1)}, bf16[2,128,512]{2,1,0:T(8,128)(2,1)S(1)}, u32[]{:S(2)}, u32[]{:S(2)}) collective-permute-start(bf16[2,128,512]{2,1,0:T(8,128)(2,1)} %bitcast.65), channel_id=1, source_target_pairs={{0,8},{8,16},{16,24},{24,0},{1,9},{9,17},{17,25},{25,1},{2,10},{10... | collective-permute-start | bytes 786440 | tf_op jit(solution)/shard_map/ppermute | solution.py:36
  3.0 13.6 %collective-permute-start.1 = (bf16[2,128,512]{2,1,0:T(8,128)(2,1)}, bf16[2,128,512]{2,1,0:T(8,128)(2,1)S(1)}, u32[]{:S(2)}, u32[]{:S(2)}) collective-permute-start(bf16[2,128,512]{2,1,0:T(8,128)(2,1)} %bitcast.66), channel_id=1, source_target_pairs={{0,24},{8,0},{16,8},{24,16},{1,25},{9,1},{17,9},{25,17},{2,26},{10... | collective-permute-start | bytes 786440 | tf_op jit(solution)/shard_map/ppermute | solution.py:41
  8.0 36.7 %all-to-all-start = ((s32[8,1,1]{2,1,0:T(1,128)}), s32[8,1,1]{2,1,0:T(1,128)S(1)}, u32[]{:S(2)}, u32[]{:S(2)}) async-start(s32[8,1,1]{2,1,0:T(1,128)} %copy.23), calls=%async_computation | async-start | bytes 8192 | tf_op jit(solution)/shard_map/all_to_all | solution.py:61
  15.0 10.6 %collective-permute-start.2 = (bf16[2,128,512]{2,1,0:T(8,128)(2,1)S(1)}, bf16[2,128,512]{2,1,0:T(8,128)(2,1)S(1)}, u32[]{:S(2)}, u32[]{:S(2)}) collective-permute-start(bf16[2,128,512]{2,1,0:T(8,128)(2,1)S(1)} %collective-permute-done), channel_id=1, source_target_pairs={{0,8},{8,16},{16,24},{24,0},{1,9},{9,17},{17,25},{25,1},{2,10},{10... | collective-permute-start | bytes 786440 | tf_op jit(solution)/shard_map/ppermute | solution.py:36
  44.7 20.2 %copy-start.1 = (bf16[512,512]{1,0:T(8,128)(2,1)S(1)}, bf16[512,512]{1,0:T(8,128)(2,1)}, u32[]{:S(2)}) copy-start(bf16[512,512]{1,0:T(8,128)(2,1)} %param.12) | copy-start | bytes 1572868
  44.7 19.4 %all-to-all-start.1 = ((bf16[8,128,512]{2,1,0:T(8,128)(2,1)}), bf16[8,128,512]{2,1,0:T(8,128)(2,1)S(1)}, u32[]{:S(2)}, u32[]{:S(2)}) async-start(bf16[8,128,512]{2,1,0:T(8,128)(2,1)} %copy.26), calls=%async_computation.1 | async-start | bytes 2097152 | tf_op jit(solution)/shard_map/all_to_all | solution.py:58
  65.2 11.2 %collective-permute-start.3 = (bf16[2,128,512]{2,1,0:T(8,128)(2,1)S(1)}, bf16[2,128,512]{2,1,0:T(8,128)(2,1)S(1)}, u32[]{:S(2)}, u32[]{:S(2)}) collective-permute-start(bf16[2,128,512]{2,1,0:T(8,128)(2,1)S(1)} %bitcast.60), channel_id=1, source_target_pairs={{0,8},{8,16},{16,24},{24,0},{1,9},{9,17},{17,25},{25,1},{2,10},{10... | collective-permute-start | bytes 786440 | tf_op jit(solution)/shard_map/ppermute | solution.py:36
  65.2 13.0 %collective-permute-start.4 = (bf16[2,128,512]{2,1,0:T(8,128)(2,1)S(1)}, bf16[2,128,512]{2,1,0:T(8,128)(2,1)S(1)}, u32[]{:S(2)}, u32[]{:S(2)}) collective-permute-start(bf16[2,128,512]{2,1,0:T(8,128)(2,1)S(1)} %bitcast.61), channel_id=1, source_target_pairs={{0,24},{8,0},{16,8},{24,16},{1,25},{9,1},{17,9},{25,17},{2,26},{10... | collective-permute-start | bytes 786440 | tf_op jit(solution)/shard_map/ppermute | solution.py:41
  76.4 8.2 %collective-permute-start.5 = (bf16[2,128,512]{2,1,0:T(8,128)(2,1)S(1)}, bf16[2,128,512]{2,1,0:T(8,128)(2,1)S(1)}, u32[]{:S(2)}, u32[]{:S(2)}) collective-permute-start(bf16[2,128,512]{2,1,0:T(8,128)(2,1)S(1)} %collective-permute-done.3), channel_id=1, source_target_pairs={{0,8},{8,16},{16,24},{24,0},{1,9},{9,17},{17,25},{25,1},{2,10},{10... | collective-permute-start | bytes 786440 | tf_op jit(solution)/shard_map/ppermute | solution.py:36
  102.7 19.9 %copy-start.2 = (bf16[512,512]{1,0:T(8,128)(2,1)S(1)}, bf16[512,512]{1,0:T(8,128)(2,1)}, u32[]{:S(2)}) copy-start(bf16[512,512]{1,0:T(8,128)(2,1)} %param.13) | copy-start | bytes 1572868
